TPU v7x, 32 devices: a whole 2x2x4 slice. The times are simulated.
32 devices in a mesh: layer: 2 (over core), prow: 4 (over z), pcol: 4 (over y, x).
Axes of the slice: x: 2, y: 2, z: 4, core: 2. Of those that a mesh axis runs over, the one named last changes fastest.
Arguments:
- factor: bfloat16 [2, 4, 4, 4, 4, 256, 256], P('layer', 'prow', None, None, 'pcol'), may hold values from -0.1875 to 0.1875
- factor_scale: float32 [2, 4, 4, 4, 4], P('layer', 'prow', None, None, 'pcol'), may hold values from 0.25 to 4
- sub_pattern: int32 [2, 4, 4, 4, 4], P('layer', 'prow', None, None, 'pcol'), may hold values from 0 to 1, as said below
- coupling: bfloat16 [2, 4, 4, 4, 4, 256, 256], P('layer', 'prow', None, None, 'pcol'), may hold values from -0.1875 to 0.1875
- coupling_scale: float32 [2, 4, 4, 4, 4], P('layer', 'prow', None, None, 'pcol'), may hold values from 0.25 to 4
- top_pattern: int32 [2, 4, 4, 4, 4], P('layer', 'prow', None, None, 'pcol'), may hold values 0 or 1
- diag_inverse: float32 [2, 4, 4, 256, 256], P('layer', 'prow', 'pcol'), may hold values from -1 to 2
- top_inverse: float32 [4, 4, 256, 256], P('prow', 'pcol'), may hold values from -1 to 2
- rhs_sub: float32 [2, 4, 4, 256, 256], P('layer', 'prow', 'pcol'), may hold values from -6 to 6
- rhs_top: float32 [4, 4, 256, 256], P('prow', 'pcol'), may hold values from -6 to 6
Outputs:
- sol_sub: float32 [2, 4, 4, 256, 256], P('layer', 'prow', 'pcol')
- sol_top: float32 [4, 4, 256, 256], P('prow', 'pcol')
Inputs may be any that keep to these rules, and one draw needn't show every extreme that they name: The supernodes of each layer fall into 3 levels; sub_pattern is 1 only where the column supernode's level is below the row supernode's level.
All inputs are finite; a program needn't handle non-finite values. No bound on the sum of `top_pattern` on one device may be relied on, other than what follows from the above.
Results may differ from a plain program's by a relative error of at most 0.02.
Values may be sent and summed in bfloat16 or wider, within the bound.
No kernel may reach another device: no remote copies, remote signals or barrier semaphores. Data moves between devices by JAX's collectives and lax.ppermute only.
A program may use at most 64 MiB of HBM per device.

v0:
```python
import jax
import jax.numpy as jnp
from jax import lax
from jax.sharding import PartitionSpec as P

LEVELS = 3
HIGH_PREC = lax.Precision.HIGHEST


def apply_left(matrix, values):
    return jnp.dot(matrix, values, precision=HIGH_PREC, preferred_element_type=jnp.float32)


def apply_trans(matrix, values):
    return jnp.dot(matrix.T, values, precision=HIGH_PREC, preferred_element_type=jnp.float32)


def forward_partial(values, matrices, scaling):
    shared = values.astype(jnp.bfloat16)[None]
    products = jnp.einsum(
        "bawk,akr->bawr",
        matrices,
        lax.all_gather(shared, "prow", axis=0, tiled=True),
        preferred_element_type=jnp.float32,
    )
    return jnp.sum(products * scaling[:, :, None, None], axis=1)


def column_total(values, matrices, scaling):
    shared = values.astype(jnp.bfloat16)[None]
    products = jnp.einsum(
        "bakw,bkr->bawr",
        matrices,
        lax.all_gather(shared, "pcol", axis=0, tiled=True),
        preferred_element_type=jnp.float32,
    )
    partial_value = jnp.sum(products * scaling[:, :, None, None], axis=0)
    return lax.psum_scatter(
        partial_value.astype(jnp.bfloat16), "prow", scatter_dimension=0, tiled=True
    ).astype(jnp.float32)[0]


def shards(
    factor,
    factor_scale,
    sub_pattern,
    coupling,
    coupling_scale,
    top_pattern,
    diag_inverse,
    top_inverse,
    rhs_sub,
    rhs_top,
):
    super_width = factor.shape[5]
    row_count = factor.shape[2]
    col_count = factor.shape[3]
    factor_blocks = factor.reshape(row_count, col_count, super_width, super_width)
    factor_weights = (factor_scale * sub_pattern.astype(jnp.float32)).reshape(row_count, col_count)
    link_blocks = coupling.reshape(row_count, col_count, super_width, super_width)
    link_weights = (coupling_scale * top_pattern.astype(jnp.float32)).reshape(row_count, col_count)
    inverse = diag_inverse.reshape(super_width, super_width)
    top_matrix = top_inverse.reshape(super_width, super_width)
    own_rhs = rhs_sub.reshape(super_width, rhs_sub.shape[-1])
    top_rhs = rhs_top.reshape(super_width, rhs_top.shape[-1])
    solved = apply_left(inverse, own_rhs)
    for sweep_index in range(LEVELS - 1):
        partial_value = forward_partial(solved, factor_blocks, factor_weights)
        lower_sum = lax.psum_scatter(
            partial_value.astype(jnp.bfloat16), "pcol", scatter_dimension=0, tiled=True
        ).astype(jnp.float32)[0]
        solved = apply_left(inverse, own_rhs - lower_sum)
    top_partial = forward_partial(solved, link_blocks, link_weights)
    top_part = lax.psum_scatter(
        top_partial.astype(jnp.bfloat16), "pcol", scatter_dimension=0, tiled=True
    ).astype(jnp.float32)[0]
    merged = lax.psum(top_part.astype(jnp.bfloat16), "layer").astype(jnp.float32)
    top_fwd = apply_left(top_matrix, top_rhs - merged)
    top_answer = apply_trans(top_matrix, top_fwd)
    coupled = column_total(top_answer, link_blocks, link_weights)
    answer = apply_trans(inverse, solved - coupled)
    for sweep_index in range(LEVELS - 1):
        upper_sum = column_total(answer, factor_blocks, factor_weights)
        answer = apply_trans(inverse, solved - coupled - upper_sum)
    return (answer.reshape(rhs_sub.shape), top_answer.reshape(rhs_top.shape))


def solution(mesh):
    return jax.shard_map(
        shards,
        mesh=mesh,
        in_specs=(
            P("layer", "prow", None, None, "pcol", None, None),
            P("layer", "prow", None, None, "pcol"),
            P("layer", "prow", None, None, "pcol"),
            P("layer", "prow", None, None, "pcol", None, None),
            P("layer", "prow", None, None, "pcol"),
            P("layer", "prow", None, None, "pcol"),
            P("layer", "prow", "pcol", None, None),
            P("prow", "pcol", None, None),
            P("layer", "prow", "pcol", None, None),
            P("prow", "pcol", None, None),
        ),
        out_specs=(P("layer", "prow", "pcol", None, None), P("prow", "pcol", None, None)),
        check_vma=False,
    )
```

profile of v0, /device:TPU:0, one launch (start us, length us, event | category | flops | bytes accessed | tf_op | source)
XLA Modules:
  0.0 298.1 jit_solution(12780264937894898415)
XLA Ops:
  7.2 0.0 reduce-scatter.19.cloned.1.call-start
  7.2 0.8 convert_multiply_fusion.1
  8.1 0.1 copy.27
  8.2 1.4 convolution_convert_fusion.3
  9.6 17.4 %all-gather = bf16[1024,256]{1,0:T(8,128)(2,1)S(1)} all-gather(bf16[256,256]{1,0:T(8,128)(2,1)S(1)} %convolution_convert_fusion.3), channel_id=2, replica_groups=mesh['layer'=2,'prow'=4,'pcol'=4] {'prow'}, dimensions={0}, use_global_device_ids=true | all-gather | bytes 655360 | tf_op jit(solution)/shard_map/all_gather | solution.py:23
  27.0 0.9 fusion.2
  27.9 1.0 copy.28
  28.9 0.0 reduce-scatter.21.cloned.1.call-start
  28.9 27.0 %reduce-scatter.19.cloned.1.call-done = bf16[1,256,256]{2,1,0:T(8,128)(2,1)} async-done(((bf16[4,256,256]{2,1,0:T(8,128)(2,1)}), bf16[1,256,256]{2,1,0:T(8,128)(2,1)}) %reduce-scatter.19.cloned.1.call-update) | async-done | bytes 131088
  55.9 1.5 fusion.6
  57.4 15.4 %all-gather.1 = bf16[1024,256]{0,1:T(8,128)(2,1)S(1)} all-gather(bf16[256,256]{0,1:T(8,128)(2,1)S(1)} %fusion.6), channel_id=3, replica_groups=mesh['layer'=2,'prow'=4,'pcol'=4] {'prow'}, dimensions={0}, use_global_device_ids=true | all-gather | bytes 655360 | tf_op jit(solution)/shard_map/all_gather | solution.py:23
  72.8 1.2 reshape.51
  74.0 1.9 fusion.1
  75.9 1.0 copy.31
  76.8 0.0 reduce-scatter.21.cloned.1.call-update
  76.9 0.0 reduce-scatter.23.cloned.1.call-start
  77.0 0.1 copy.34
  77.0 25.9 %reduce-scatter.21.cloned.1.call-done = bf16[1,256,256]{2,1,0:T(8,128)(2,1)} async-done(((bf16[4,256,256]{2,1,0:T(8,128)(2,1)}), bf16[1,256,256]{2,1,0:T(8,128)(2,1)}) %reduce-scatter.21.cloned.1.call-update) | async-done | bytes 131088
  102.9 1.5 fusion.37
  104.4 15.4 %all-gather.2 = bf16[1024,256]{0,1:T(8,128)(2,1)S(1)} all-gather(bf16[256,256]{0,1:T(8,128)(2,1)S(1)} %get-tuple-element.6), channel_id=4, replica_groups=mesh['layer'=2,'prow'=4,'pcol'=4] {'prow'}, dimensions={0}, use_global_device_ids=true | all-gather | bytes 655360 | tf_op jit(solution)/shard_map/all_gather | solution.py:23
  119.8 1.2 reshape.52
  121.0 3.5 %fusion = bf16[4,256,256]{1,2,0:T(8,128)(2,1)} fusion(f32[4,4]{0,1:T(4,128)S(1)} %copy.34, bf16[4,256,256,1]{1,0,2,3:T(4,128)(2,1)} %bitcast.158, bf16[1,1,4,4,1,256,256]{6,5,4,3,2,1,0:T(8,128)(2,1)} %param.13), kind=kOutput, calls=%fused_computation.1 | convolution fusion | flops 538705920 | bytes 3145792 | tf_op jit(solution)/shard_map/bawk,akr->bawr/dot_general | solution.py:20
  124.5 2.1 copy.35
  126.5 0.0 all-reduce.5.cloned.1.call-start
  126.6 26.0 %reduce-scatter.23.cloned.1.call-done = bf16[1,256,256]{2,1,0:T(8,128)(2,1)} async-done(((bf16[4,256,256]{2,1,0:T(8,128)(2,1)}), bf16[1,256,256]{2,1,0:T(8,128)(2,1)}) %reduce-scatter.23.cloned.1.call-update) | async-done | bytes 131088
  152.6 0.0 reduce-scatter.13.cloned.1.call-start
  152.7 20.1 %all-reduce.5.cloned.1.call-done = bf16[256,256]{1,0:T(8,128)(2,1)} async-done(((bf16[256,256]{1,0:T(8,128)(2,1)}), bf16[256,256]{1,0:T(8,128)(2,1)}) %all-reduce.5.cloned.1.call-update) | async-done | bytes 131088 | tf_op jit(solution)/shard_map/psum | solution.py:77
  172.7 1.5 fusion.20
  174.2 0.4 bitcast_convert_fusion
  174.6 14.6 %all-gather.3 = bf16[1024,256]{0,1:T(8,128)(2,1)S(1)} all-gather(bf16[256,256]{0,1:T(8,128)(2,1)S(1)} %get-tuple-element.8), channel_id=5, replica_groups=mesh['layer'=2,'prow'=4,'pcol'=4] {'pcol'}, dimensions={0}, use_global_device_ids=true | all-gather | bytes 655360 | tf_op jit(solution)/shard_map/all_gather | solution.py:34
  189.2 1.2 reshape.53
  190.4 3.4 %multiply_reduce_fusion.2 = bf16[256,4,256]{2,0,1:T(8,128)(2,1)} fusion(f32[4,4]{1,0:T(4,128)S(1)} %bitcast.167, bf16[4,256,256,1]{1,0,2,3:T(4,128)(2,1)} %bitcast.159, bf16[1,1,4,4,1,256,256]{6,5,4,3,2,1,0:T(8,128)(2,1)} %param.13), kind=kOutput, calls=%fused_computation.8 | convolution fusion | flops 538705920 | bytes 3145792 | tf_op jit(solution)/shard_map/bakw,bkr->bawr/dot_general | solution.py:31
  193.8 0.0 reduce-scatter.15.cloned.1.call-start
  193.9 22.0 %reduce-scatter.13.cloned.1.call-done = bf16[1,256,256]{1,2,0:T(8,128)(2,1)} async-done(((bf16[4,256,256]{1,2,0:T(8,128)(2,1)}), bf16[1,256,256]{1,2,0:T(8,128)(2,1)}) %reduce-scatter.13.cloned.1.call-update) | async-done | bytes 131088 | tf_op jit(solution)/shard_map/reduce_scatter | solution.py:38
  215.8 1.3 fusion.7
  217.1 12.0 %all-gather.4 = bf16[1024,256]{0,1:T(8,128)(2,1)S(1)} all-gather(bf16[256,256]{0,1:T(8,128)(2,1)S(1)} %fusion.7), channel_id=6, replica_groups=mesh['layer'=2,'prow'=4,'pcol'=4] {'pcol'}, dimensions={0}, use_global_device_ids=true | all-gather | bytes 655360 | tf_op jit(solution)/shard_map/all_gather | solution.py:34
  229.1 1.2 reshape.54
  230.3 2.7 multiply_reduce_fusion.1
  233.0 0.0 reduce-scatter.17.cloned.1.call-start
  233.1 19.4 %reduce-scatter.15.cloned.1.call-done = bf16[1,256,256]{1,2,0:T(8,128)(2,1)} async-done(((bf16[4,256,256]{1,2,0:T(8,128)(2,1)}), bf16[1,256,256]{1,2,0:T(8,128)(2,1)}) %reduce-scatter.15.cloned.1.call-update) | async-done | bytes 131088 | tf_op jit(solution)/shard_map/reduce_scatter | solution.py:38
  252.4 1.3 fusion.8
  253.7 12.0 %all-gather.5 = bf16[1024,256]{0,1:T(8,128)(2,1)S(1)} all-gather(bf16[256,256]{0,1:T(8,128)(2,1)S(1)} %fusion.8), channel_id=7, replica_groups=mesh['layer'=2,'prow'=4,'pcol'=4] {'pcol'}, dimensions={0}, use_global_device_ids=true | all-gather | bytes 655360 | tf_op jit(solution)/shard_map/all_gather | solution.py:34
  265.8 1.2 reshape.55
  267.0 2.7 multiply_reduce_fusion
  269.7 0.8 copy.40
  270.5 18.6 %reduce-scatter.17.cloned.1.call-done = bf16[1,256,256]{1,2,0:T(8,128)(2,1)} async-done(((bf16[4,256,256]{1,2,0:T(8,128)(2,1)}), bf16[1,256,256]{1,2,0:T(8,128)(2,1)}) %reduce-scatter.17.cloned.1.call-update) | async-done | bytes 131088 | tf_op jit(solution)/shard_map/reduce_scatter | solution.py:38
  289.1 1.3 convolution_bitcast_fusion
  290.4 0.8 copy.39
  (23 shorter events, 0.1 us)
Async XLA Ops:
  7.2 19.8 %copy-start = (bf16[1,1,4,4,1,256,256]{6,5,4,3,2,1,0:T(8,128)(2,1)S(1)}, bf16[1,1,4,4,1,256,256]{6,5,4,3,2,1,0:T(8,128)(2,1)}, u32[]{:S(2)}) copy-start(bf16[1,1,4,4,1,256,256]{6,5,4,3,2,1,0:T(8,128)(2,1)} %param.10) | copy-start | bytes 6291460
  7.2 48.7 %reduce-scatter.19.cloned.1.call-start = ((), (), s32[]{:S(2)}) async-start(), calls=%async_computation.10 | async-start | bytes 655360
  27.0 29.0 %copy-start.1 = (f32[1,1,1,256,256]{4,3,2,1,0:T(8,128)S(1)}, f32[1,1,1,256,256]{4,3,2,1,0:T(8,128)}, u32[]{:S(2)}) copy-start(f32[1,1,1,256,256]{4,3,2,1,0:T(8,128)} %param.16) | copy-start | bytes 786436
  27.0 29.0 %copy-start.2 = (f32[1,1,1,256,256]{4,3,2,1,0:T(8,128)S(1)}, f32[1,1,1,256,256]{4,3,2,1,0:T(8,128)}, u32[]{:S(2)}) copy-start(f32[1,1,1,256,256]{4,3,2,1,0:T(8,128)} %param.18) | copy-start | bytes 786436
  28.9 74.0 %reduce-scatter.21.cloned.1.call-start = ((), (), s32[]{:S(2)}) async-start(), calls=%async_computation.11 | async-start | bytes 655360
  74.0 2.9 copy-start.6
  74.0 3.0 copy-start.7
  76.9 75.7 %reduce-scatter.23.cloned.1.call-start = ((), (), s32[]{:S(2)}) async-start(), calls=%async_computation.12 | async-start | bytes 655360
  121.0 51.7 %copy-start.4 = (f32[1,1,256,256]{3,2,1,0:T(8,128)S(1)}, f32[1,1,256,256]{3,2,1,0:T(8,128)}, u32[]{:S(2)}) copy-start(f32[1,1,256,256]{3,2,1,0:T(8,128)} %param.17) | copy-start | bytes 786436
  121.0 51.7 %copy-start.5 = (f32[1,1,256,256]{3,2,1,0:T(8,128)S(1)}, f32[1,1,256,256]{3,2,1,0:T(8,128)}, u32[]{:S(2)}) copy-start(f32[1,1,256,256]{3,2,1,0:T(8,128)} %param.19) | copy-start | bytes 786436
  126.5 46.2 %all-reduce.5.cloned.1.call-start = ((), (), s32[]{:S(2)}) async-start(), calls=%async_computation.6 | async-start | bytes 262144 | tf_op jit(solution)/shard_map/psum | solution.py:77
  152.6 63.2 %reduce-scatter.13.cloned.1.call-start = ((), (), s32[]{:S(2)}) async-start(), calls=%async_computation.7 | async-start | bytes 655360 | tf_op jit(solution)/shard_map/reduce_scatter | solution.py:38
  193.8 58.6 %reduce-scatter.15.cloned.1.call-start = ((), (), s32[]{:S(2)}) async-start(), calls=%async_computation.8 | async-start | bytes 655360 | tf_op jit(solution)/shard_map/reduce_scatter | solution.py:38
  230.3 22.1 %copy-start.3 = (bf16[1,256,256]{1,2,0:T(8,128)(2,1)S(1)}, bf16[1,256,256]{1,2,0:T(8,128)(2,1)}, u32[]{:S(2)}) copy-start(bf16[1,256,256]{1,2,0:T(8,128)(2,1)} %reduce-scatter.13.cloned.1.call-done) | copy-start | bytes 393220
  233.0 56.1 %reduce-scatter.17.cloned.1.call-start = ((), (), s32[]{:S(2)}) async-start(), calls=%async_computation.9 | async-start | bytes 655360 | tf_op jit(solution)/shard_map/reduce_scatter | solution.py:38
Sparse Core Ops, SparseCore 0:
  29.0 26.8 reduce-scatter.18
  77.0 25.8 reduce-scatter.20
  126.7 25.8 reduce-scatter.22
  154.7 17.9 all-reduce.4
  193.9 21.8 reduce-scatter.12
  233.1 19.2 reduce-scatter.14
  269.8 19.2 reduce-scatter.16
where the time goes:
time: 299 us; the launch traced here: 298 us
  waiting for transfers between devices  159 us (53%)
  blocking collectives  86.8 us (29%)
  matrix products  25.1 us (8%)
  between operations  14.2 us (5%)
  local copies, waits for them, and re-layouts  11.8 us (4%)
    unnamed x10, waiting for transfers between devices  78.9 us
    reduce_scatter x3, waiting for transfers between devices, column_total(): lax.psum_scatter(partial_value.astype(jnp.bfloat16), 'prow', scatter_dime...  59.9 us
    all_gather x3, blocking collectives, forward_partial(): lax.all_gather(shared, 'prow', axis=0, tiled=True)  48.2 us
    all_gather x3, blocking collectives, column_total(): lax.all_gather(shared, 'pcol', axis=0, tiled=True)  38.7 us
    psum x1, waiting for transfers between devices, shards(): lax.psum(top_part.astype(jnp.bfloat16), 'layer').astype(jnp.float32)  20.1 us
    dot_general x3, matrix products, column_total(): jnp.einsum('bakw,bkr->bawr', matrices, lax.all_gather(shared, 'pcol', axi...  8.74 us
    dot_general x3, matrix products, forward_partial(): jnp.einsum('bawk,akr->bawr', matrices, lax.all_gather(shared, 'prow', axi...  6.24 us
  transfers between devices with their start and end apart: 7, of which 7 were waited for; matrix products, arithmetic and copies ran while one was open for 0% of the time, Pallas kernels for 0%

commit v1 on v0

--- a/solution.py
+++ b/solution.py
@@ -5,6 +5,11 @@
 
 LEVELS = 3
 HIGH_PREC = lax.Precision.HIGHEST
+
+
+def _feed_points(vec):
+    z_new = lax.all_gather(vec, axis_name="layer")
+    return jnp.sum(z_new, 0)
 
 
 def apply_left(matrix, values):
@@ -74,7 +79,7 @@
     top_part = lax.psum_scatter(
         top_partial.astype(jnp.bfloat16), "pcol", scatter_dimension=0, tiled=True
     ).astype(jnp.float32)[0]
-    merged = lax.psum(top_part.astype(jnp.bfloat16), "layer").astype(jnp.float32)
+    merged = _feed_points(top_part.astype(jnp.bfloat16)).astype(jnp.float32)
     top_fwd = apply_left(top_matrix, top_rhs - merged)
     top_answer = apply_trans(top_matrix, top_fwd)
     coupled = column_total(top_answer, link_blocks, link_weights)

time: 299 us -> 279 us (0.933)
  waiting for transfers between devices: 159 us -> 139 us
    psum x1 -> x0, waiting for transfers between devices: 20.1 us -> none  [shards(): lax.psum(top_part.astype(jnp.bfloat16), 'layer').astype(jnp.float32)]
    unnamed x10 -> x9, waiting for transfers between devices: 78.9 us -> 78.9 us
  transfers between devices with their start and end apart: 7 -> 6, of which waited for: 7 -> 6; matrix products, arithmetic and copies ran while one was open for 0% -> 0% of each run, Pallas kernels for 0% -> 0%
where the time goes in v1:
time: 279 us
  waiting for transfers between devices  139 us (50%)
  blocking collectives  88.5 us (32%)
  matrix products  24.2 us (9%)
  between operations  14.2 us (5%)
  local copies, waits for them, and re-layouts  11.9 us (4%)
    unnamed x9, waiting for transfers between devices  78.9 us
    reduce_scatter x3, waiting for transfers between devices, column_total(): lax.psum_scatter(partial_value.astype(jnp.bfloat16), 'prow', scatter_dime...  59.9 us
    all_gather x3, blocking collectives, forward_partial(): lax.all_gather(shared, 'prow', axis=0, tiled=True)  48.2 us
    all_gather x3, blocking collectives, column_total(): lax.all_gather(shared, 'pcol', axis=0, tiled=True)  38.2 us
    dot_general x3, matrix products, column_total(): jnp.einsum('bakw,bkr->bawr', matrices, lax.all_gather(shared, 'pcol', axi...  8.74 us
    dot_general x3, matrix products, forward_partial(): jnp.einsum('bawk,akr->bawr', matrices, lax.all_gather(shared, 'prow', axi...  6.21 us
  transfers between devices with their start and end apart: 6, of which 6 were waited for; matrix products, arithmetic and copies ran while one was open for 0% of the time, Pallas kernels for 0%

profile of v1, /device:TPU:0, one launch (start us, length us, event | category | flops | bytes accessed | tf_op | source)
XLA Modules:
  0.0 278.8 jit_solution(9389369926255821906)
XLA Ops:
  7.2 0.0 reduce-scatter.19.cloned.1.call-start
  7.2 0.8 convert_multiply_fusion.1
  8.1 0.1 copy.27
  8.2 1.4 convolution_convert_fusion.3
  9.6 17.4 %all-gather = bf16[1024,256]{1,0:T(8,128)(2,1)S(1)} all-gather(bf16[256,256]{1,0:T(8,128)(2,1)S(1)} %convolution_convert_fusion.3), channel_id=2, replica_groups=mesh['layer'=2,'prow'=4,'pcol'=4] {'prow'}, dimensions={0}, use_global_device_ids=true | all-gather | bytes 655360 | tf_op jit(solution)/shard_map/all_gather | solution.py:28
  27.0 0.9 fusion.2
  27.9 1.0 copy.28
  28.9 0.0 reduce-scatter.21.cloned.1.call-start
  28.9 27.0 %reduce-scatter.19.cloned.1.call-done = bf16[1,256,256]{2,1,0:T(8,128)(2,1)} async-done(((bf16[4,256,256]{2,1,0:T(8,128)(2,1)}), bf16[1,256,256]{2,1,0:T(8,128)(2,1)}) %reduce-scatter.19.cloned.1.call-update) | async-done | bytes 131088
  55.9 1.5 fusion.6
  57.4 15.4 %all-gather.1 = bf16[1024,256]{0,1:T(8,128)(2,1)S(1)} all-gather(bf16[256,256]{0,1:T(8,128)(2,1)S(1)} %fusion.6), channel_id=3, replica_groups=mesh['layer'=2,'prow'=4,'pcol'=4] {'prow'}, dimensions={0}, use_global_device_ids=true | all-gather | bytes 655360 | tf_op jit(solution)/shard_map/all_gather | solution.py:28
  72.8 1.2 reshape.58
  74.0 1.9 fusion.1
  75.9 1.0 copy.31
  76.8 0.0 reduce-scatter.21.cloned.1.call-update
  76.9 0.0 reduce-scatter.23.cloned.1.call-start
  77.0 0.1 copy.34
  77.0 25.9 %reduce-scatter.21.cloned.1.call-done = bf16[1,256,256]{2,1,0:T(8,128)(2,1)} async-done(((bf16[4,256,256]{2,1,0:T(8,128)(2,1)}), bf16[1,256,256]{2,1,0:T(8,128)(2,1)}) %reduce-scatter.21.cloned.1.call-update) | async-done | bytes 131088
  102.9 1.5 fusion.39
  104.4 15.4 %all-gather.2 = bf16[1024,256]{0,1:T(8,128)(2,1)S(1)} all-gather(bf16[256,256]{0,1:T(8,128)(2,1)S(1)} %get-tuple-element.6), channel_id=4, replica_groups=mesh['layer'=2,'prow'=4,'pcol'=4] {'prow'}, dimensions={0}, use_global_device_ids=true | all-gather | bytes 655360 | tf_op jit(solution)/shard_map/all_gather | solution.py:28
  119.8 1.2 reshape.59
  121.0 3.4 %fusion = bf16[4,256,256]{1,2,0:T(8,128)(2,1)} fusion(f32[4,4]{0,1:T(4,128)S(1)} %copy.34, bf16[4,256,256,1]{1,0,2,3:T(4,128)(2,1)} %bitcast.163, bf16[1,1,4,4,1,256,256]{6,5,4,3,2,1,0:T(8,128)(2,1)} %param.13), kind=kOutput, calls=%fused_computation.1 | convolution fusion | flops 538705920 | bytes 3145792 | tf_op jit(solution)/shard_map/bawk,akr->bawr/dot_general | solution.py:25
  124.4 2.1 copy.35
  126.6 0.0 reduce-scatter.13.cloned.1.call-start
  126.6 26.0 %reduce-scatter.23.cloned.1.call-done = bf16[1,256,256]{2,1,0:T(8,128)(2,1)} async-done(((bf16[4,256,256]{2,1,0:T(8,128)(2,1)}), bf16[1,256,256]{2,1,0:T(8,128)(2,1)}) %reduce-scatter.23.cloned.1.call-update) | async-done | bytes 131088
  152.6 2.2 all_gather.25
  154.9 0.6 fusion.15
  155.5 0.4 bitcast_convert_fusion
  155.9 14.1 %all-gather.3 = bf16[1024,256]{0,1:T(8,128)(2,1)S(1)} all-gather(bf16[256,256]{0,1:T(8,128)(2,1)S(1)} %get-tuple-element.8), channel_id=5, replica_groups=mesh['layer'=2,'prow'=4,'pcol'=4] {'pcol'}, dimensions={0}, use_global_device_ids=true | all-gather | bytes 655360 | tf_op jit(solution)/shard_map/all_gather | solution.py:39
  170.0 1.2 reshape.60
  171.1 3.4 %multiply_reduce_fusion.2 = bf16[256,4,256]{2,0,1:T(8,128)(2,1)} fusion(f32[4,4]{1,0:T(4,128)S(1)} %bitcast.171, bf16[4,256,256,1]{1,0,2,3:T(4,128)(2,1)} %bitcast.164, bf16[1,1,4,4,1,256,256]{6,5,4,3,2,1,0:T(8,128)(2,1)} %param.13), kind=kOutput, calls=%fused_computation.8 | convolution fusion | flops 538705920 | bytes 3145792 | tf_op jit(solution)/shard_map/bakw,bkr->bawr/dot_general | solution.py:36
  174.6 0.0 reduce-scatter.15.cloned.1.call-start
  174.6 21.9 %reduce-scatter.13.cloned.1.call-done = bf16[1,256,256]{1,2,0:T(8,128)(2,1)} async-done(((bf16[4,256,256]{1,2,0:T(8,128)(2,1)}), bf16[1,256,256]{1,2,0:T(8,128)(2,1)}) %reduce-scatter.13.cloned.1.call-update) | async-done | bytes 131088 | tf_op jit(solution)/shard_map/reduce_scatter | solution.py:43
  196.5 1.3 fusion.7
  197.8 12.0 %all-gather.4 = bf16[1024,256]{0,1:T(8,128)(2,1)S(1)} all-gather(bf16[256,256]{0,1:T(8,128)(2,1)S(1)} %fusion.7), channel_id=6, replica_groups=mesh['layer'=2,'prow'=4,'pcol'=4] {'pcol'}, dimensions={0}, use_global_device_ids=true | all-gather | bytes 655360 | tf_op jit(solution)/shard_map/all_gather | solution.py:39
  209.9 1.2 reshape.61
  211.0 2.7 multiply_reduce_fusion.1
  213.7 0.0 reduce-scatter.15.cloned.1.call-update
  213.7 0.0 reduce-scatter.17.cloned.1.call-start
  213.8 19.4 %reduce-scatter.15.cloned.1.call-done = bf16[1,256,256]{1,2,0:T(8,128)(2,1)} async-done(((bf16[4,256,256]{1,2,0:T(8,128)(2,1)}), bf16[1,256,256]{1,2,0:T(8,128)(2,1)}) %reduce-scatter.15.cloned.1.call-update) | async-done | bytes 131088 | tf_op jit(solution)/shard_map/reduce_scatter | solution.py:43
  233.2 1.3 fusion.8
  234.5 12.1 %all-gather.5 = bf16[1024,256]{0,1:T(8,128)(2,1)S(1)} all-gather(bf16[256,256]{0,1:T(8,128)(2,1)S(1)} %fusion.8), channel_id=7, replica_groups=mesh['layer'=2,'prow'=4,'pcol'=4] {'pcol'}, dimensions={0}, use_global_device_ids=true | all-gather | bytes 655360 | tf_op jit(solution)/shard_map/all_gather | solution.py:39
  246.6 1.2 reshape.62
  247.7 2.7 multiply_reduce_fusion
  250.4 0.8 copy.40
  251.3 18.6 %reduce-scatter.17.cloned.1.call-done = bf16[1,256,256]{1,2,0:T(8,128)(2,1)} async-done(((bf16[4,256,256]{1,2,0:T(8,128)(2,1)}), bf16[1,256,256]{1,2,0:T(8,128)(2,1)}) %reduce-scatter.17.cloned.1.call-update) | async-done | bytes 131088 | tf_op jit(solution)/shard_map/reduce_scatter | solution.py:43
  269.8 1.3 convolution_bitcast_fusion
  271.1 0.8 copy.39
  (22 shorter events, 0.2 us)
Async XLA Ops:
  7.2 19.8 %copy-start = (bf16[1,1,4,4,1,256,256]{6,5,4,3,2,1,0:T(8,128)(2,1)S(1)}, bf16[1,1,4,4,1,256,256]{6,5,4,3,2,1,0:T(8,128)(2,1)}, u32[]{:S(2)}) copy-start(bf16[1,1,4,4,1,256,256]{6,5,4,3,2,1,0:T(8,128)(2,1)} %param.10) | copy-start | bytes 6291460
  7.2 48.7 %reduce-scatter.19.cloned.1.call-start = ((), (), s32[]{:S(2)}) async-start(), calls=%async_computation.9 | async-start | bytes 655360
  27.0 29.0 %copy-start.1 = (f32[1,1,1,256,256]{4,3,2,1,0:T(8,128)S(1)}, f32[1,1,1,256,256]{4,3,2,1,0:T(8,128)}, u32[]{:S(2)}) copy-start(f32[1,1,1,256,256]{4,3,2,1,0:T(8,128)} %param.16) | copy-start | bytes 786436
  27.0 29.0 %copy-start.2 = (f32[1,1,1,256,256]{4,3,2,1,0:T(8,128)S(1)}, f32[1,1,1,256,256]{4,3,2,1,0:T(8,128)}, u32[]{:S(2)}) copy-start(f32[1,1,1,256,256]{4,3,2,1,0:T(8,128)} %param.18) | copy-start | bytes 786436
  28.9 74.0 %reduce-scatter.21.cloned.1.call-start = ((), (), s32[]{:S(2)}) async-start(), calls=%async_computation.10 | async-start | bytes 655360
  74.0 2.9 %copy-start.6 = (f32[1,1,4,4,1]{3,4,2,1,0:T(1,128)S(1)}, f32[1,1,4,4,1]{3,4,2,1,0:T(1,128)}, u32[]{:S(2)}) copy-start(f32[1,1,4,4,1]{3,4,2,1,0:T(1,128)} %param.14) | copy-start | bytes 196
  74.0 3.0 %copy-start.7 = (s32[1,1,4,4,1]{3,4,2,1,0:T(1,128)S(1)}, s32[1,1,4,4,1]{3,4,2,1,0:T(1,128)}, u32[]{:S(2)}) copy-start(s32[1,1,4,4,1]{3,4,2,1,0:T(1,128)} %param.15) | copy-start | bytes 196
  76.9 75.7 %reduce-scatter.23.cloned.1.call-start = ((), (), s32[]{:S(2)}) async-start(), calls=%async_computation.11 | async-start | bytes 655360
  124.4 30.4 %copy-start.4 = (f32[1,1,256,256]{3,2,1,0:T(8,128)S(1)}, f32[1,1,256,256]{3,2,1,0:T(8,128)}, u32[]{:S(2)}) copy-start(f32[1,1,256,256]{3,2,1,0:T(8,128)} %param.17) | copy-start | bytes 786436
  124.4 30.4 %copy-start.5 = (f32[1,1,256,256]{3,2,1,0:T(8,128)S(1)}, f32[1,1,256,256]{3,2,1,0:T(8,128)}, u32[]{:S(2)}) copy-start(f32[1,1,256,256]{3,2,1,0:T(8,128)} %param.19) | copy-start | bytes 786436
  126.6 70.0 %reduce-scatter.13.cloned.1.call-start = ((), (), s32[]{:S(2)}) async-start(), calls=%async_computation.6 | async-start | bytes 655360 | tf_op jit(solution)/shard_map/reduce_scatter | solution.py:43
  174.6 58.6 %reduce-scatter.15.cloned.1.call-start = ((), (), s32[]{:S(2)}) async-start(), calls=%async_computation.7 | async-start | bytes 655360 | tf_op jit(solution)/shard_map/reduce_scatter | solution.py:43
  211.0 22.1 %copy-start.3 = (bf16[1,256,256]{1,2,0:T(8,128)(2,1)S(1)}, bf16[1,256,256]{1,2,0:T(8,128)(2,1)}, u32[]{:S(2)}) copy-start(bf16[1,256,256]{1,2,0:T(8,128)(2,1)} %reduce-scatter.13.cloned.1.call-done) | copy-start | bytes 393220
  213.7 56.1 %reduce-scatter.17.cloned.1.call-start = ((), (), s32[]{:S(2)}) async-start(), calls=%async_computation.8 | async-start | bytes 655360 | tf_op jit(solution)/shard_map/reduce_scatter | solution.py:43
Sparse Core Ops, SparseCore 0:
  29.0 26.8 reduce-scatter.18
  77.0 25.8 reduce-scatter.20
  126.7 25.8 reduce-scatter.22
  174.7 21.8 reduce-scatter.12
  213.9 19.2 reduce-scatter.14
  250.6 19.2 reduce-scatter.16
